TPU v7x, 32 devices: a whole 2x2x4 slice. The times are simulated.
32 devices in a mesh: parts: 2 (over y), vocab: 4 (over z), mp: 2 (over x), rep: 2 (over core).
Axes of the slice: x: 2, y: 2, z: 4, core: 2. Of those that a mesh axis runs over, the one named last changes fastest.
Arguments:
- resid_base: bfloat16 [128, 4608], P(('parts', 'vocab', 'rep'), 'mp'), parts along dimension 0, may hold values from -60 to 60
- mlp_hidden: bfloat16 [128, 36864], P(('parts', 'vocab', 'rep'), 'mp'), parts along dimension 0, may hold values from -6 to 6
- edit_in: float32 [73728], P(('parts', 'mp')), parts along dimension 0, may hold values from -0.03125 to 0.03125
- edit_out: float32 [9216], P(('parts', 'mp')), parts along dimension 0, may hold values from -6 to 6
- norm_gain: float32 [4608], P('mp'), may hold values from 0.5 to 1.5
- head: bfloat16 [4608, 8192], P(None, ('vocab', 'mp', 'rep')), may hold values from -0.25 to 0.25
- token_ids: int32 [128], P('parts'), parts along dimension 0, may hold values from 0 to 8191
Outputs:
- penalty: float32 [128], P(('parts', 'vocab', 'rep')), parts along dimension 0
- grad_in: float32 [73728], P(('parts', 'mp')), parts along dimension 0
- grad_out: float32 [9216], P(('parts', 'mp')), parts along dimension 0
There are 2 independent parts, one for each index of `parts`. A program takes and returns all parts, laid end to end along the dimension named above; an argument that names none is the same for every part. Nothing has to cross between parts.
All inputs are finite; a program needn't handle non-finite values.
Results may differ from a plain program's by a relative error of at most 0.011.
Values may be sent and summed in bfloat16 or wider, within the bound.
No kernel may reach another device: no remote copies, remote signals or barrier semaphores. Data moves between devices by JAX's collectives and lax.ppermute only.
A program may use at most 64 MiB of HBM per device.

v0:
```python
import jax
import jax.numpy as jnp
from jax import lax
from jax.sharding import PartitionSpec as P

D = 4608
softcap = 30.0
epsilon = 1e-06


def local(resid_base, mlp_hidden, edit_in, edit_out, norm_gain, head, token_ids):
    tok_rows = resid_base.shape[0]
    feat_cols = resid_base.shape[1]
    voc_cols = head.shape[1]
    hidden_f = mlp_hidden.astype(jnp.float32)
    base_f = resid_base.astype(jnp.float32)
    mix_part = jnp.sum(hidden_f * edit_in[None, :], axis=1)
    mix_scale, square_base, base_along, out_square = lax.psum(
        (
            mix_part,
            jnp.sum(base_f * base_f, axis=1),
            jnp.sum(base_f * edit_out[None, :], axis=1),
            jnp.sum(edit_out * edit_out),
        ),
        "mp",
    )
    resid = base_f + mix_scale[:, None] * edit_out[None, :]
    square_edit = square_base + 2.0 * mix_scale * base_along + mix_scale * mix_scale * out_square
    along = base_along + mix_scale * out_square
    edit_scale = lax.rsqrt(square_edit / D + epsilon)
    base_scale = lax.rsqrt(square_base / D + epsilon)
    x_edit = (resid * edit_scale[:, None] * norm_gain[None, :]).astype(jnp.bfloat16)
    x_base = (base_f * base_scale[:, None] * norm_gain[None, :]).astype(jnp.bfloat16)
    stacked = jnp.stack([x_edit, x_base], axis=0)
    direction = lax.all_gather(edit_out * norm_gain, "mp", axis=0, tiled=True)
    weights_all = lax.all_gather(mix_scale * edit_scale, ("vocab", "rep"), axis=0, tiled=True)
    full_cols = lax.all_gather(stacked, "mp", axis=2, tiled=True)
    logits_pre = jnp.einsum(
        "ktd,dv->ktv",
        lax.all_gather(full_cols, ("vocab", "rep"), axis=1, tiled=True),
        head,
        preferred_element_type=jnp.float32,
    )
    capped = softcap * jnp.tanh(logits_pre / softcap)
    totals = lax.psum(jnp.sum(jnp.exp(capped), axis=2), ("vocab", "mp", "rep"))
    log_totals = jnp.log(totals)
    probs = jnp.exp(capped - log_totals[:, :, None])
    z_edit = capped[0]
    z_base = capped[1]
    first_col = lax.axis_index(("vocab", "mp", "rep")) * voc_cols
    columns = first_col + jnp.arange(voc_cols, dtype=jnp.int32)
    onehot = (token_ids[:, None] == columns[None, :]).astype(jnp.float32)
    diff = z_base - z_edit
    kl_part = jnp.sum(probs[1] * diff, axis=1)
    gap_part = jnp.sum(onehot * diff, axis=1)
    dy_rows = ((2.0 * probs[0] - probs[1] - onehot) * (1.0 - (z_edit / softcap) ** 2)).astype(
        jnp.bfloat16
    )
    dx_part = lax.dot_general(
        dy_rows, head, (((1,), (1,)), ((), ())), preferred_element_type=jnp.float32
    )
    align_part = jnp.sum(logits_pre[0] * dy_rows.astype(jnp.float32), axis=1)
    proj_part = jnp.dot(dx_part, direction, precision=lax.Precision.HIGHEST)
    weighted_part = jnp.dot(weights_all, dx_part, precision=lax.Precision.HIGHEST)
    kl_all, gap_all, proj_all, align_all, weighted_all = lax.psum(
        (kl_part, gap_part, proj_part, align_part, weighted_part), ("vocab", "mp", "rep")
    )
    tok_start = lax.axis_index(("vocab", "rep")) * tok_rows
    feat_start = lax.axis_index("mp") * feat_cols
    kl_own = lax.dynamic_slice_in_dim(kl_all, tok_start, tok_rows, 0)
    gap_own = lax.dynamic_slice_in_dim(gap_all, tok_start, tok_rows, 0)
    proj_own = lax.dynamic_slice_in_dim(proj_all, tok_start, tok_rows, 0)
    align_own = lax.dynamic_slice_in_dim(align_all, tok_start, tok_rows, 0)
    lse_own = lax.dynamic_slice_in_dim(log_totals, tok_start, tok_rows, 1)
    penalty = kl_own + gap_own + 2.0 * (lse_own[0] - lse_own[1])
    normed = resid * edit_scale[:, None]
    shrink = edit_scale * align_own / D
    coeff = edit_scale * proj_own - shrink * (edit_scale * along)
    second_part = jnp.sum((mix_scale * shrink)[:, None] * normed, axis=0)
    grad_in_part = jnp.sum(coeff[:, None] * hidden_f, axis=0)
    second_sum, grad_in = lax.psum((second_part, grad_in_part), ("vocab", "rep"))
    weighted_own = lax.dynamic_slice_in_dim(weighted_all, feat_start, feat_cols, 0)
    grad_out = norm_gain * weighted_own - second_sum
    return (penalty, grad_in, grad_out)


def solution(mesh):
    in_specs = (
        P(("parts", "vocab", "rep"), "mp"),
        P(("parts", "vocab", "rep"), "mp"),
        P(("parts", "mp")),
        P(("parts", "mp")),
        P("mp"),
        P(None, ("vocab", "mp", "rep")),
        P("parts"),
    )
    out_specs = (P(("parts", "vocab", "rep")), P(("parts", "mp")), P(("parts", "mp")))
    return jax.shard_map(local, mesh=mesh, in_specs=in_specs, out_specs=out_specs, check_vma=False)
```

profile of v0, /device:TPU:8, one launch (start us, length us, event | category | flops | bytes accessed | tf_op | source)
XLA Modules:
  0.0 234.1 jit_solution(15880379331970252911)
XLA Ops:
  7.2 0.0 all-gather.3.cloned.1.call-start
  7.2 1.3 fusion.23
  8.6 0.9 fusion.15
  9.5 1.2 fusion.2
  10.7 1.2 dynamic-slice
  12.6 5.6 %all-reduce.2 = (f32[8]{0:T(128)S(1)}, f32[8]{0:T(128)S(1)}, f32[8]{0:T(128)S(1)}, f32[]{:T(128)}) all-reduce(f32[8]{0:T(128)S(1)} %get-tuple-element.6, f32[8]{0:T(128)S(1)} %fusion.2, f32[8]{0:T(128)S(1)} %get-tuple-element.5, f32[]{:T(128)} %get-tuple-element.26), channel_id=1, replica_groups=mesh['parts'=2,'vocab'=4,'mp'=2,'rep'=2] {'mp'}, use_global_device_ids=true, to_apply=%region_3.0 | all-reduce | flops 25 | bytes 200 | tf_op jit(solution)/shard_map/psum | solution.py:18
  18.2 0.7 multiply_dynamic-update-slice_fusion
  19.0 0.9 fusion.18
  19.9 5.1 %all_gather.12 = bf16[2,8,4608]{2,1,0:T(8,128)(2,1)} all-gather(bf16[2,8,2304]{2,1,0:T(8,128)(2,1)S(1)} %pad_maximum_fusion), channel_id=1, replica_groups=mesh['parts'=2,'vocab'=4,'mp'=2,'rep'=2] {'mp'}, dimensions={2}, use_global_device_ids=true | all-gather | bytes 221184 | tf_op jit(solution)/shard_map/all_gather | solution.py:37
  25.0 0.0 all-gather.3.cloned.1.call-update
  25.0 0.0 all-reduce.5.cloned.1.call-start
  25.1 10.7 %all-reduce = f32[64]{0:T(128)S(1)} all-reduce(f32[64]{0:T(128)S(1)} %get-tuple-element.15), channel_id=1, replica_groups=mesh['parts'=2,'vocab'=4,'mp'=2,'rep'=2] {'vocab','rep'}, use_global_device_ids=true, to_apply=%add | all-reduce | flops 64 | bytes 512
  35.8 4.4 %all-gather = f32[2,1,2304]{2,1,0:T(1,128)S(1)} all-gather(f32[1,1,2304]{2,1,0:T(1,128)S(1)} %reshape.34), channel_id=1, replica_groups=mesh['parts'=2,'vocab'=4,'mp'=2,'rep'=2] {'mp'}, dimensions={0}, use_global_device_ids=true | all-gather | bytes 27648 | tf_op jit(solution)/shard_map/all_gather | solution.py:35
  40.2 9.0 %all-gather.3.cloned.1.call-done = bf16[2,64,4608]{2,1,0:T(8,128)(2,1)} async-done(((bf16[2,8,4608]{2,1,0:T(8,128)(2,1)}), bf16[2,64,4608]{2,1,0:T(8,128)(2,1)}) %all-gather.3.cloned.1.call-update) | async-done | bytes 1179664 | tf_op jit(solution)/shard_map/all_gather | solution.py:40
  49.2 3.6 %exponential_reduce_fusion = (f32[2,64]{1,0:T(2,128)S(1)}, f32[2,64,512]{2,1,0:T(8,128)S(1)}) fusion(bf16[2,64,4608]{2,1,0:T(8,128)(2,1)} %all-gather.3.cloned.1.call-done, bf16[4608,512]{1,0:T(8,128)(2,1)} %param.12), kind=kOutput, calls=%fused_computation.9 | convolution fusion | flops 604176256 | bytes 6160896 | tf_op jit(solution)/shard_map/ktd,dv->ktv/dot_general | solution.py:38
  52.8 24.3 %psum.88 = f32[2,64]{1,0:T(2,128)S(1)} all-reduce(f32[2,64]{1,0:T(2,128)S(1)} %get-tuple-element.30), channel_id=1, replica_groups=mesh['parts'=2,'vocab'=4,'mp'=2,'rep'=2] {'vocab','mp','rep'}, use_global_device_ids=true, to_apply=%region_9.0 | all-reduce | flops 128 | bytes 1024 | tf_op jit(solution)/shard_map/psum | solution.py:45
  77.1 0.1 subtract_exponential_fusion
  77.2 0.2 fusion.9
  77.4 3.9 %fusion.24 = f32[64,4608]{1,0:T(8,128)S(1)} fusion(bf16[64,512]{1,0:T(8,128)(2,1)S(1)} %get-tuple-element.18, bf16[4608,512]{1,0:T(8,128)(2,1)} %param.12), kind=kOutput, calls=%fused_computation.54 | convolution fusion | flops 301989888 | bytes 5963776 | tf_op jit(solution)/shard_map/dot_general | solution.py:59
  81.3 0.7 convolution_reduce_fusion
  82.0 1.0 convolution_bitcast_fusion
  83.1 0.1 constant_dynamic-slice_fusion
  83.1 57.7 %all-reduce.1 = (f32[64]{0:T(128)S(1)}, f32[64]{0:T(128)S(1)}, f32[64]{0:T(128)S(1)}, f32[4608]{0:T(1024)S(1)}) all-reduce(f32[64]{0:T(128)S(1)} %add.92, f32[64]{0:T(128)S(1)} %convolution_bitcast_fusion, f32[64]{0:T(128)S(1)} %get-tuple-element.17, ...), channel_id=1, replica_groups=mesh['parts'=2,'vocab'=4,'mp'=2,'rep'=2] {'vocab','mp','rep'}, use_global_device_ids=true, to_apply=%region_11.0 | all-reduce | flops 4800 | bytes 38400 | tf_op jit(solution)/shard_map/psum | solution.py:65
  140.8 0.7 fusion.21
  141.5 0.1 multiply_reduce_fusion.1
  141.6 30.3 %psum.95 = f32[2304]{0:T(1024)S(1)} all-reduce(f32[2304]{0:T(1024)S(1)} %multiply_reduce_fusion.1), channel_id=1, replica_groups=mesh['parts'=2,'vocab'=4,'mp'=2,'rep'=2] {'vocab','rep'}, use_global_device_ids=true, to_apply=%region_21.0 | all-reduce | flops 2304 | bytes 18432 | tf_op jit(solution)/shard_map/psum | solution.py:81
  171.9 1.0 fusion.3
  172.9 0.0 all-reduce.5.cloned.1.call-update
  173.0 0.7 multiply_subtract_fusion
  173.6 0.6 bitcast_add_fusion
  174.2 51.5 %all-reduce.5.cloned.1.call-done = f32[18432]{0:T(1024)} async-done(((f32[18432]{0:T(1024)}), f32[18432]{0:T(1024)}) %all-reduce.5.cloned.1.call-update) | async-done | bytes 73744 | tf_op jit(solution)/shard_map/psum | solution.py:81
  225.7 1.5 copy.12
  (16 shorter events, 0.1 us)
Async XLA Ops:
  7.2 42.0 %all-gather.3.cloned.1.call-start = ((), (), s32[]{:S(2)}) async-start(), calls=%async_computation | async-start | bytes 1327104 | tf_op jit(solution)/shard_map/all_gather | solution.py:40
  25.0 200.7 %all-reduce.5.cloned.1.call-start = ((), (), s32[]{:S(2)}) async-start(), calls=%async_computation.1 | async-start | bytes 147456 | tf_op jit(solution)/shard_map/psum | solution.py:81
  40.2 37.0 %copy-start.4 = (s32[64]{0:T(128)S(1)}, s32[64]{0:T(128)}, u32[]{:S(2)}) copy-start(s32[64]{0:T(128)} %param.13) | copy-start | bytes 772
  81.3 60.2 %copy-start.1 = (bf16[8,2304]{1,0:T(8,128)(2,1)S(1)}, bf16[8,2304]{1,0:T(8,128)(2,1)}, u32[]{:S(2)}) copy-start(bf16[8,2304]{1,0:T(8,128)(2,1)} %param.7) | copy-start | bytes 110596
  81.3 60.2 %copy-start.2 = (f32[2304]{0:T(1024)S(1)}, f32[2304]{0:T(1024)}, u32[]{:S(2)}) copy-start(f32[2304]{0:T(1024)} %param.10) | copy-start | bytes 27652
  81.3 90.6 %copy-start = (bf16[8,18432]{1,0:T(8,128)(2,1)S(1)}, bf16[8,18432]{1,0:T(8,128)(2,1)}, u32[]{:S(2)}) copy-start(bf16[8,18432]{1,0:T(8,128)(2,1)} %param.8) | copy-start | bytes 884740
  82.0 90.9 %copy-start.3 = (f32[2304]{0:T(1024)S(1)}, f32[2304]{0:T(1024)}, u32[]{:S(2)}) copy-start(f32[2304]{0:T(1024)} %param.11) | copy-start | bytes 27652
Sparse Core Ops, SparseCore 0:
  25.1 24.0 all-gather.2
  173.1 52.6 all-reduce.4
where the time goes:
time: 235 us; the launch traced here: 234 us
  blocking collectives  138 us (59%)
  waiting for transfers between devices  60.5 us (26%)
  between operations  14.8 us (6%)
  matrix products  9.18 us (4%)
  other arithmetic  8.58 us (4%)
  local copies, waits for them, and re-layouts  2.88 us (1%)
    psum x1, blocking collectives, local(): lax.psum((kl_part, gap_part, proj_part, align_part, weighted_part), ('voc...  57.7 us
    psum x1, waiting for transfers between devices, local(): lax.psum((second_part, grad_in_part), ('vocab', 'rep'))  51.5 us
    psum x1, blocking collectives, local(): lax.psum((second_part, grad_in_part), ('vocab', 'rep'))  30.3 us
    psum x1, blocking collectives, local(): totals = lax.psum(jnp.sum(jnp.exp(capped), axis=2), ('vocab', 'mp', 'rep'))  24.3 us
    unnamed x1, blocking collectives  10.7 us
    all_gather x1, waiting for transfers between devices, local(): lax.all_gather(full_cols, ('vocab', 'rep'), axis=1, tiled=True)  9 us
    psum x1, blocking collectives, local(): lax.psum((mix_part, jnp.sum(base_f * base_f, axis=1), jnp.sum(base_f * ed...  5.58 us
    all_gather x1, blocking collectives, local(): full_cols = lax.all_gather(stacked, 'mp', axis=2, tiled=True)  5.14 us
  transfers between devices with their start and end apart: 2, of which 2 were waited for; matrix products, arithmetic and copies ran while one was open for 1% of the time, Pallas kernels for 0%

commit v1 on v0

--- a/solution.py
+++ b/solution.py
@@ -42,7 +42,8 @@
         preferred_element_type=jnp.float32,
     )
     capped = softcap * jnp.tanh(logits_pre / softcap)
-    totals = lax.psum(jnp.sum(jnp.exp(capped), axis=2), ("vocab", "mp", "rep"))
+    field = jnp.sum(jnp.exp(capped), axis=2)
+    totals = lax.all_gather(field, ("vocab", "mp", "rep")).sum(axis=0)
     log_totals = jnp.log(totals)
     probs = jnp.exp(capped - log_totals[:, :, None])
     z_edit = capped[0]

time: 235 us -> 223 us (0.949)
  blocking collectives: 138 us -> 126 us
    psum x1 -> x0, blocking collectives: 24.3 us -> none  [local(): totals = lax.psum(jnp.sum(jnp.exp(capped), axis=2), ('vocab', 'mp', 'rep'))]
    all_gather x0 -> x1, blocking collectives: none -> 17.2 us  [local(): totals = lax.all_gather(field, ('vocab', 'mp', 'rep')).sum(axis=0)]
    psum x1, blocking collectives: 57.7 us -> 52.6 us  [local(): lax.psum((kl_part, gap_part, proj_part, align_part, weighted_part), ('voc...]
where the time goes in v1:
time: 223 us; the launch traced here: 222 us
  blocking collectives  126 us (57%)
  waiting for transfers between devices  60.5 us (27%)
  between operations  14.8 us (7%)
  matrix products  9.18 us (4%)
  other arithmetic  8.6 us (4%)
  local copies, waits for them, and re-layouts  2.88 us (1%)
    psum x1, blocking collectives, local(): lax.psum((kl_part, gap_part, proj_part, align_part, weighted_part), ('voc...  52.6 us
    psum x1, waiting for transfers between devices, local(): lax.psum((second_part, grad_in_part), ('vocab', 'rep'))  51.5 us
    psum x1, blocking collectives, local(): lax.psum((second_part, grad_in_part), ('vocab', 'rep'))  30.3 us
    all_gather x1, blocking collectives, local(): totals = lax.all_gather(field, ('vocab', 'mp', 'rep')).sum(axis=0)  17.2 us
    unnamed x1, blocking collectives  10.7 us
    all_gather x1, waiting for transfers between devices, local(): lax.all_gather(full_cols, ('vocab', 'rep'), axis=1, tiled=True)  9 us
    psum x1, blocking collectives, local(): lax.psum((mix_part, jnp.sum(base_f * base_f, axis=1), jnp.sum(base_f * ed...  5.58 us
    all_gather x1, blocking collectives, local(): full_cols = lax.all_gather(stacked, 'mp', axis=2, tiled=True)  5.14 us
  transfers between devices with their start and end apart: 2, of which 2 were waited for; matrix products, arithmetic and copies ran while one was open for 1% of the time, Pallas kernels for 0%

profile of v1, /device:TPU:8, one launch (start us, length us, event | category | flops | bytes accessed | tf_op | source)
XLA Modules:
  0.0 222.0 jit_solution(4937958762853988680)
XLA Ops:
  7.2 0.0 all-gather.5.cloned.1.call-start
  7.2 1.3 fusion.23
  8.6 0.9 fusion.15
  9.5 1.2 fusion.2
  10.7 1.2 dynamic-slice
  12.6 5.6 %all-reduce.2 = (f32[8]{0:T(128)S(1)}, f32[8]{0:T(128)S(1)}, f32[8]{0:T(128)S(1)}, f32[]{:T(128)}) all-reduce(f32[8]{0:T(128)S(1)} %get-tuple-element.6, f32[8]{0:T(128)S(1)} %fusion.2, f32[8]{0:T(128)S(1)} %get-tuple-element.5, f32[]{:T(128)} %get-tuple-element.26), channel_id=1, replica_groups=mesh['parts'=2,'vocab'=4,'mp'=2,'rep'=2] {'mp'}, use_global_device_ids=true, to_apply=%region_3.0 | all-reduce | flops 25 | bytes 200 | tf_op jit(solution)/shard_map/psum | solution.py:18
  18.2 0.7 multiply_dynamic-update-slice_fusion
  19.0 0.9 fusion.18
  19.9 5.1 %all_gather.18 = bf16[2,8,4608]{2,1,0:T(8,128)(2,1)} all-gather(bf16[2,8,2304]{2,1,0:T(8,128)(2,1)S(1)} %pad_maximum_fusion), channel_id=1, replica_groups=mesh['parts'=2,'vocab'=4,'mp'=2,'rep'=2] {'mp'}, dimensions={2}, use_global_device_ids=true | all-gather | bytes 221184 | tf_op jit(solution)/shard_map/all_gather | solution.py:37
  25.0 0.0 all-gather.5.cloned.1.call-update
  25.0 0.0 all-reduce.5.cloned.1.call-start
  25.1 10.7 %all-reduce = f32[64]{0:T(128)S(1)} all-reduce(f32[64]{0:T(128)S(1)} %get-tuple-element.15), channel_id=1, replica_groups=mesh['parts'=2,'vocab'=4,'mp'=2,'rep'=2] {'vocab','rep'}, use_global_device_ids=true, to_apply=%add | all-reduce | flops 64 | bytes 512
  35.8 4.4 %all-gather.2 = f32[2,1,2304]{2,1,0:T(1,128)S(1)} all-gather(f32[1,1,2304]{2,1,0:T(1,128)S(1)} %reshape.39), channel_id=1, replica_groups=mesh['parts'=2,'vocab'=4,'mp'=2,'rep'=2] {'mp'}, dimensions={0}, use_global_device_ids=true | all-gather | bytes 27648 | tf_op jit(solution)/shard_map/all_gather | solution.py:35
  40.2 9.0 %all-gather.5.cloned.1.call-done = bf16[2,64,4608]{2,1,0:T(8,128)(2,1)} async-done(((bf16[2,8,4608]{2,1,0:T(8,128)(2,1)}), bf16[2,64,4608]{2,1,0:T(8,128)(2,1)}) %all-gather.5.cloned.1.call-update) | async-done | bytes 1179664 | tf_op jit(solution)/shard_map/all_gather | solution.py:40
  49.2 3.6 %exponential_reduce_fusion = (f32[2,64]{1,0:T(2,128)S(1)}, f32[2,64,512]{2,1,0:T(8,128)S(1)}) fusion(bf16[2,64,4608]{2,1,0:T(8,128)(2,1)} %all-gather.5.cloned.1.call-done, bf16[4608,512]{1,0:T(8,128)(2,1)} %param.12), kind=kOutput, calls=%fused_computation.9 | convolution fusion | flops 604176256 | bytes 6160896 | tf_op jit(solution)/shard_map/ktd,dv->ktv/dot_general | solution.py:38
  52.8 17.2 %all-gather.1 = f32[16,2,64]{2,1,0:T(2,128)S(1)} all-gather(f32[1,2,64]{2,1,0:T(2,128)S(1)} %bitcast.55), channel_id=2, replica_groups=mesh['parts'=2,'vocab'=4,'mp'=2,'rep'=2] {'vocab','mp','rep'}, dimensions={0}, use_global_device_ids=true | all-gather | bytes 8704 | tf_op jit(solution)/shard_map/all_gather | solution.py:46
  70.1 0.1 subtract_exponential_fusion
  70.2 0.2 fusion.9
  70.4 3.9 %fusion.24 = f32[64,4608]{1,0:T(8,128)S(1)} fusion(bf16[64,512]{1,0:T(8,128)(2,1)S(1)} %get-tuple-element.18, bf16[4608,512]{1,0:T(8,128)(2,1)} %param.12), kind=kOutput, calls=%fused_computation.54 | convolution fusion | flops 301989888 | bytes 5963776 | tf_op jit(solution)/shard_map/dot_general | solution.py:60
  74.3 0.7 convolution_reduce_fusion
  75.0 1.0 convolution_bitcast_fusion
  76.1 0.1 constant_dynamic-slice_fusion
  76.1 52.6 %all-reduce.1 = (f32[64]{0:T(128)S(1)}, f32[64]{0:T(128)S(1)}, f32[64]{0:T(128)S(1)}, f32[4608]{0:T(1024)S(1)}) all-reduce(f32[64]{0:T(128)S(1)} %add.90, f32[64]{0:T(128)S(1)} %convolution_bitcast_fusion, f32[64]{0:T(128)S(1)} %get-tuple-element.17, ...), channel_id=1, replica_groups=mesh['parts'=2,'vocab'=4,'mp'=2,'rep'=2] {'vocab','mp','rep'}, use_global_device_ids=true, to_apply=%region_11.0 | all-reduce | flops 4800 | bytes 38400 | tf_op jit(solution)/shard_map/psum | solution.py:66
  128.8 0.7 fusion.21
  129.5 0.1 multiply_reduce_fusion.1
  129.6 30.3 %psum.87 = f32[2304]{0:T(1024)S(1)} all-reduce(f32[2304]{0:T(1024)S(1)} %multiply_reduce_fusion.1), channel_id=1, replica_groups=mesh['parts'=2,'vocab'=4,'mp'=2,'rep'=2] {'vocab','rep'}, use_global_device_ids=true, to_apply=%region_21.0 | all-reduce | flops 2304 | bytes 18432 | tf_op jit(solution)/shard_map/psum | solution.py:82
  159.9 1.0 fusion.3
  160.9 0.0 all-reduce.5.cloned.1.call-update
  160.9 0.7 multiply_subtract_fusion
  161.6 0.6 bitcast_add_fusion
  162.2 51.5 %all-reduce.5.cloned.1.call-done = f32[18432]{0:T(1024)} async-done(((f32[18432]{0:T(1024)}), f32[18432]{0:T(1024)}) %all-reduce.5.cloned.1.call-update) | async-done | bytes 73744 | tf_op jit(solution)/shard_map/psum | solution.py:82
  213.7 1.5 copy.12
  (17 shorter events, 0.1 us)
Async XLA Ops:
  7.2 42.0 %all-gather.5.cloned.1.call-start = ((), (), s32[]{:S(2)}) async-start(), calls=%async_computation | async-start | bytes 1327104 | tf_op jit(solution)/shard_map/all_gather | solution.py:40
  25.0 188.7 %all-reduce.5.cloned.1.call-start = ((), (), s32[]{:S(2)}) async-start(), calls=%async_computation.1 | async-start | bytes 147456 | tf_op jit(solution)/shard_map/psum | solution.py:82
  40.2 30.0 %copy-start.4 = (s32[64]{0:T(128)S(1)}, s32[64]{0:T(128)}, u32[]{:S(2)}) copy-start(s32[64]{0:T(128)} %param.13) | copy-start | bytes 772
  74.3 55.2 %copy-start.1 = (bf16[8,2304]{1,0:T(8,128)(2,1)S(1)}, bf16[8,2304]{1,0:T(8,128)(2,1)}, u32[]{:S(2)}) copy-start(bf16[8,2304]{1,0:T(8,128)(2,1)} %param.7) | copy-start | bytes 110596
  74.3 55.2 %copy-start.2 = (f32[2304]{0:T(1024)S(1)}, f32[2304]{0:T(1024)}, u32[]{:S(2)}) copy-start(f32[2304]{0:T(1024)} %param.10) | copy-start | bytes 27652
  74.3 85.6 %copy-start = (bf16[8,18432]{1,0:T(8,128)(2,1)S(1)}, bf16[8,18432]{1,0:T(8,128)(2,1)}, u32[]{:S(2)}) copy-start(bf16[8,18432]{1,0:T(8,128)(2,1)} %param.8) | copy-start | bytes 884740
  75.0 85.9 %copy-start.3 = (f32[2304]{0:T(1024)S(1)}, f32[2304]{0:T(1024)}, u32[]{:S(2)}) copy-start(f32[2304]{0:T(1024)} %param.11) | copy-start | bytes 27652
Sparse Core Ops, SparseCore 0:
  25.1 24.0 all-gather.4
  161.0 52.6 all-reduce.4
